TPU v7x, 32 devices: a whole 2x2x4 slice. The times are simulated.
32 devices in a mesh: layer: 2 (over x), row: 4 (over y, core), col: 4 (over z).
Axes of the slice: x: 2, y: 2, z: 4, core: 2. Of those that a mesh axis runs over, the one named last changes fastest.
Arguments:
- down_source: float32 [2, 64, 4096], P('layer', None, ('row', 'col')), may hold values from -3 to 3
- up_source: float32 [2, 64, 4096], P('layer', None, ('row', 'col')), may hold values from -3 to 3
- down_transfer: bfloat16 [2, 4096, 4, 1024], P('layer', 'row', None, 'col'), may hold values from -0.09375 to 0.09375
- up_transfer: bfloat16 [2, 4096, 4, 1024], P('layer', 'row', None, 'col'), may hold values from -0.09375 to 0.09375
- reflection: bfloat16 [2, 4096, 4, 1024], P('layer', 'row', None, 'col'), may hold values from -0.09375 to 0.09375
Outputs:
- traces: float32 [2, 64, 4096], P('layer', None, ('row', 'col'))
All inputs are finite; a program needn't handle non-finite values.
Results may differ from a plain program's by a relative error of at most 0.015.
Values may be sent and summed in bfloat16 or wider, within the bound.
A program may use at most 64 MiB of HBM per device.

v0:
```python
import jax
import jax.numpy as jnp
from jax import lax
from jax.sharding import PartitionSpec as P


def for_sending(value):

    def short(part):
        return part.astype(jnp.bfloat16) if part.dtype == jnp.float32 else part

    return jax.tree.map(short, value)


def passed_along(block, axis, distance):
    devices = range(lax.axis_size(axis))
    route = [(i - distance, i) for i in devices if i - distance in devices]
    return lax.ppermute(block, axis, route)


def contract(data_rows, matrix_rows):
    return lax.dot_general(
        data_rows, matrix_rows, (((1,), (1,)), ((), ())), preferred_element_type=jnp.float32
    )


def on_device(down_source, up_source, down_transfer, up_transfer, reflection):
    height = down_transfer.shape[1]
    down_tile = down_transfer[0].reshape(height, -1)
    up_tile = up_transfer[0].reshape(height, -1)
    reflect_tile = reflection[0].reshape(height, -1)
    own_down = down_source[0]
    own_up = up_source[0]
    layer_count = lax.axis_size("layer")

    def sweep_product(inputs):
        pieces = jax.tree.map(
            lambda a: lax.all_gather(a, "row", axis=1, tiled=True), for_sending(inputs)
        )
        return (
            lax.psum_scatter(
                contract(pieces[0], down_tile), "col", scatter_dimension=1, tiled=True
            ),
            lax.psum_scatter(contract(pieces[1], up_tile), "col", scatter_dimension=1, tiled=True),
        )

    def send_both(down_now, up_now):
        from_below = passed_along(down_now, "layer", 1)
        from_above = passed_along(up_now, "layer", -1)
        return sweep_product((from_below, from_above))

    def round_update(counter, carried):
        down_now, up_now = carried
        down_gain, up_gain = send_both(down_now.astype(jnp.bfloat16), up_now.astype(jnp.bfloat16))
        return (own_down + down_gain, own_up + up_gain)

    down_all, up_all = lax.fori_loop(0, layer_count - 1, round_update, (own_down, own_up))
    summed = down_all + up_all
    mixed_trace = summed.astype(jnp.bfloat16)
    running = contract(lax.all_gather(mixed_trace, "row", axis=1, tiled=True), reflect_tile)
    reflected = lax.psum_scatter(
        running.astype(jnp.bfloat16), "col", scatter_dimension=1, tiled=True
    ).astype(jnp.float32)
    return (summed + reflected)[None]


def solution(mesh):
    in_specs = (
        P("layer", None, ("row", "col")),
        P("layer", None, ("row", "col")),
        P("layer", "row", None, "col"),
        P("layer", "row", None, "col"),
        P("layer", "row", None, "col"),
    )
    out_specs = P("layer", None, ("row", "col"))
    return jax.shard_map(
        on_device, mesh=mesh, in_specs=in_specs, out_specs=out_specs, check_vma=False
    )
```

profile of v0, /device:TPU:0, one launch (start us, length us, event | category | flops | bytes accessed | tf_op | source)
XLA Modules:
  0.0 97.0 jit_solution(5956092463700425919)
XLA Ops:
  6.5 0.0 reduce-scatter.4.cloned.1.call-start
  6.5 0.8 bitcast_convert_fusion.1
  7.4 4.9 %collective-permute-start = (bf16[64,256]{1,0:T(8,128)(2,1)S(1)}, bf16[64,256]{1,0:T(8,128)(2,1)S(1)}, u32[]{:S(2)}, u32[]{:S(2)}) collective-permute-start(bf16[64,256]{1,0:T(8,128)(2,1)S(1)} %bitcast_convert_fusion.1), channel_id=1, source_target_pairs={{0,16},{1,17},{2,18},{3,19},{4,20},{5,21},{6,22},{7,23},{8,24},{9,... | collective-permute-start | bytes 98312 | tf_op jit(solution)/shard_map/while/body/eval_jaxpr/ppermute | solution.py:18
  12.3 2.1 %copy.6 = bf16[128,8,4,256]{3,1,2,0:T(8,128)(2,1)S(1)} copy(bf16[128,8,4,256]{3,2,1,0:T(4,128)(2,1)} %bitcast.32) | data formatting | bytes 4194304
  14.3 0.0 copy-start.2
  14.4 0.0 copy-start
  14.4 0.0 collective-permute-done
  14.4 5.5 %all_gather.11 = bf16[64,1024]{1,0:T(8,128)(2,1)S(1)} all-gather(bf16[64,256]{1,0:T(8,128)(2,1)S(1)} %collective-permute-done), channel_id=1, replica_groups=mesh['layer'=2,'row'=4,'col'=4] {'row'}, dimensions={1}, use_global_device_ids=true | all-gather | bytes 163840 | tf_op jit(solution)/shard_map/while/body/eval_jaxpr/all_gather | solution.py:38
  19.9 1.5 %fusion.3 = f32[64,1024]{1,0:T(8,128)} fusion(bf16[64,1024]{1,0:T(8,128)(2,1)S(1)} %all_gather.11, bf16[1024,1024]{1,0:T(8,128)(2,1)S(1)} %bitcast.30), kind=kOutput, calls=%fused_computation.8 | convolution fusion | flops 134217728 | bytes 2490368 | tf_op jit(solution)/shard_map/while/body/eval_jaxpr/dot_general | solution.py:22
  21.4 0.0 reduce-scatter.4.cloned.1.call-update
  21.4 0.0 reduce-scatter.6.cloned.1.call-start
  21.5 0.0 copy-done.2
  21.5 1.3 %collective-permute-start.1 = (bf16[64,256]{1,0:T(8,128)(2,1)S(1)}, bf16[64,256]{1,0:T(8,128)(2,1)S(1)}, u32[]{:S(2)}, u32[]{:S(2)}) collective-permute-start(bf16[64,256]{1,0:T(8,128)(2,1)S(1)} %bitcast_convert_fusion), channel_id=1, source_target_pairs={{16,0},{17,1},{18,2},{19,3},{20,4},{21,5},{22,6},{23,7},{24,8},{25... | collective-permute-start | bytes 98312 | tf_op jit(solution)/shard_map/while/body/eval_jaxpr/ppermute | solution.py:18
  22.8 0.0 copy-done
  22.8 0.5 copy.7
  23.3 4.0 %collective-permute-done.1 = bf16[64,256]{1,0:T(8,128)(2,1)S(1)} collective-permute-done((bf16[64,256]{1,0:T(8,128)(2,1)S(1)}, bf16[64,256]{1,0:T(8,128)(2,1)S(1)}, u32[]{:S(2)}, u32[]{:S(2)}) %collective-permute-start.1) | collective-permute-done | bytes 32800 | tf_op jit(solution)/shard_map/while/body/eval_jaxpr/ppermute | solution.py:18
  27.3 5.4 %all_gather.12 = bf16[64,1024]{1,0:T(8,128)(2,1)S(1)} all-gather(bf16[64,256]{1,0:T(8,128)(2,1)S(1)} %collective-permute-done.1), channel_id=1, replica_groups=mesh['layer'=2,'row'=4,'col'=4] {'row'}, dimensions={1}, use_global_device_ids=true | all-gather | bytes 163840 | tf_op jit(solution)/shard_map/while/body/eval_jaxpr/all_gather | solution.py:38
  32.7 1.5 %fusion.4 = f32[64,1024]{1,0:T(8,128)} fusion(bf16[64,1024]{1,0:T(8,128)(2,1)S(1)} %all_gather.12, bf16[1024,1024]{1,0:T(8,128)(2,1)S(1)} %bitcast.31), kind=kOutput, calls=%fused_computation.9 | convolution fusion | flops 134217728 | bytes 2490368 | tf_op jit(solution)/shard_map/while/body/eval_jaxpr/dot_general | solution.py:22
  34.2 0.0 reduce-scatter.6.cloned.1.call-update
  34.2 0.0 reduce-scatter.8.cloned.1.call-start
  34.2 0.0 copy-start.1
  34.3 2.1 %copy.8 = bf16[128,8,4,256]{3,1,2,0:T(8,128)(2,1)S(1)} copy(bf16[128,8,4,256]{3,2,1,0:T(4,128)(2,1)} %bitcast.34) | data formatting | bytes 4194304
  36.4 6.6 %reduce-scatter.4.cloned.1.call-done = f32[64,256]{1,0:T(8,128)} async-done(((f32[64,1024]{1,0:T(8,128)}), f32[64,256]{1,0:T(8,128)}) %reduce-scatter.4.cloned.1.call-update) | async-done | bytes 65552 | tf_op jit(solution)/shard_map/while/body/eval_jaxpr/reduce_scatter | solution.py:41
  43.0 20.5 %reduce-scatter.6.cloned.1.call-done = f32[64,256]{1,0:T(8,128)} async-done(((f32[64,1024]{1,0:T(8,128)}), f32[64,256]{1,0:T(8,128)}) %reduce-scatter.6.cloned.1.call-update) | async-done | bytes 65552 | tf_op jit(solution)/shard_map/while/body/eval_jaxpr/reduce_scatter | solution.py:44
  63.5 0.0 copy-done.1
  63.5 0.9 fusion.1
  64.4 5.4 %all_gather.13 = bf16[64,1024]{1,0:T(8,128)(2,1)S(1)} all-gather(bf16[64,256]{1,0:T(8,128)(2,1)S(1)} %get-tuple-element.17), channel_id=1, replica_groups=mesh['layer'=2,'row'=4,'col'=4] {'row'}, dimensions={1}, use_global_device_ids=true | all-gather | bytes 163840 | tf_op jit(solution)/shard_map/all_gather | solution.py:60
  69.8 1.4 %convolution_convert_fusion = bf16[64,1024]{1,0:T(8,128)(2,1)} fusion(bf16[64,1024]{1,0:T(8,128)(2,1)S(1)} %all_gather.13, bf16[1024,1024]{1,0:T(8,128)(2,1)S(1)} %bitcast.29), kind=kOutput, calls=%fused_computation | convolution fusion | flops 134283264 | bytes 2359296 | tf_op jit(solution)/shard_map/dot_general | solution.py:22
  71.2 0.0 reduce-scatter.8.cloned.1.call-update
  71.2 17.8 %reduce-scatter.8.cloned.1.call-done = bf16[64,256]{1,0:T(8,128)(2,1)} async-done(((bf16[64,1024]{1,0:T(8,128)(2,1)}), bf16[64,256]{1,0:T(8,128)(2,1)}) %reduce-scatter.8.cloned.1.call-update) | async-done | bytes 32784 | tf_op jit(solution)/shard_map/reduce_scatter | solution.py:61
  89.1 1.4 %add_bitcast_fusion = f32[1,64,256]{2,1,0:T(8,128)} fusion(f32[64,256]{1,0:T(8,128)S(1)} %get-tuple-element.18, bf16[64,256]{1,0:T(8,128)(2,1)} %reduce-scatter.8.cloned.1.call-done), kind=kLoop, calls=%fused_computation.6 | loop fusion | flops 32768 | bytes 163840 | tf_op jit(solution)/shard_map/broadcast_in_dim | solution.py:64
  (1 shorter events, 0.0 us)
Async XLA Ops:
  6.5 36.4 %reduce-scatter.4.cloned.1.call-start = ((), (), s32[]{:S(2)}) async-start(), calls=%async_computation.3 | async-start | bytes 327680 | tf_op jit(solution)/shard_map/while/body/eval_jaxpr/reduce_scatter | solution.py:41
  7.4 7.0 %collective-permute-start = (bf16[64,256]{1,0:T(8,128)(2,1)S(1)}, bf16[64,256]{1,0:T(8,128)(2,1)S(1)}, u32[]{:S(2)}, u32[]{:S(2)}) collective-permute-start(bf16[64,256]{1,0:T(8,128)(2,1)S(1)} %bitcast_convert_fusion.1), channel_id=1, source_target_pairs={{0,16},{1,17},{2,18},{3,19},{4,20},{5,21},{6,22},{7,23},{8,24},{9,... | collective-permute-start | bytes 98312 | tf_op jit(solution)/shard_map/while/body/eval_jaxpr/ppermute | solution.py:18
  14.3 7.1 %copy-start.2 = (f32[1,64,256]{2,1,0:T(8,128)S(1)}, f32[1,64,256]{2,1,0:T(8,128)}, u32[]{:S(2)}) copy-start(f32[1,64,256]{2,1,0:T(8,128)} %param.6) | copy-start | bytes 196612
  14.4 8.4 %copy-start = (bf16[1,1024,4,256]{3,2,1,0:T(4,128)(2,1)S(1)}, bf16[1,1024,4,256]{3,2,1,0:T(4,128)(2,1)}, u32[]{:S(2)}) copy-start(bf16[1,1024,4,256]{3,2,1,0:T(4,128)(2,1)} %param.8) | copy-start | bytes 6291460
  21.4 42.1 %reduce-scatter.6.cloned.1.call-start = ((), (), s32[]{:S(2)}) async-start(), calls=%async_computation.4 | async-start | bytes 327680 | tf_op jit(solution)/shard_map/while/body/eval_jaxpr/reduce_scatter | solution.py:44
  21.5 5.8 %collective-permute-start.1 = (bf16[64,256]{1,0:T(8,128)(2,1)S(1)}, bf16[64,256]{1,0:T(8,128)(2,1)S(1)}, u32[]{:S(2)}, u32[]{:S(2)}) collective-permute-start(bf16[64,256]{1,0:T(8,128)(2,1)S(1)} %bitcast_convert_fusion), channel_id=1, source_target_pairs={{16,0},{17,1},{18,2},{19,3},{20,4},{21,5},{22,6},{23,7},{24,8},{25... | collective-permute-start | bytes 98312 | tf_op jit(solution)/shard_map/while/body/eval_jaxpr/ppermute | solution.py:18
  34.2 54.9 %reduce-scatter.8.cloned.1.call-start = ((), (), s32[]{:S(2)}) async-start(), calls=%async_computation.5 | async-start | bytes 163840 | tf_op jit(solution)/shard_map/reduce_scatter | solution.py:61
  34.2 29.3 %copy-start.1 = (f32[1,64,256]{2,1,0:T(8,128)S(1)}, f32[1,64,256]{2,1,0:T(8,128)}, u32[]{:S(2)}) copy-start(f32[1,64,256]{2,1,0:T(8,128)} %param.5) | copy-start | bytes 196612
Sparse Core Ops, SparseCore 0:
  21.5 21.3 reduce-scatter.3
  45.2 18.2 reduce-scatter.5
  71.4 17.6 reduce-scatter.7
where the time goes:
time: 97.4 us; the launch traced here: 97 us
  waiting for transfers between devices  49 us (50%)
  blocking collectives  16.4 us (17%)
  between operations  13.2 us (14%)
  starting transfers between devices  6.24 us (6%)
  local copies, waits for them, and re-layouts  4.71 us (5%)
  matrix products  4.35 us (4%)
  other arithmetic  3.13 us (3%)
    reduce_scatter x1, waiting for transfers between devices, sweep_product(): lax.psum_scatter(contract(pieces[1], up_tile), 'col', scatter_dimension=1...  20.5 us
    reduce_scatter x1, waiting for transfers between devices, on_device(): lax.psum_scatter(running.astype(jnp.bfloat16), 'col', scatter_dimension=1...  17.8 us
    all_gather x2, blocking collectives, sweep_product(): lax.all_gather(a, 'row', axis=1, tiled=True)  11 us
    reduce_scatter x1, waiting for transfers between devices, sweep_product(): lax.psum_scatter(contract(pieces[0], down_tile), 'col', scatter_dimension...  6.57 us
    ppermute x2, starting transfers between devices, passed_along(): return lax.ppermute(block, axis, route)  6.15 us
    all_gather x1, blocking collectives, on_device(): lax.all_gather(mixed_trace, 'row', axis=1, tiled=True)  5.42 us
    unnamed x9, local copies, waits for them, and re-layouts  4.71 us
    dot_general x3, matrix products, contract(): lax.dot_general(data_rows, matrix_rows, (((1,), (1,)), ((), ())), preferr...  4.35 us
  transfers between devices with their start and end apart: 5, of which 4 were waited for; matrix products, arithmetic and copies ran while one was open for 6% of the time, Pallas kernels for 0%

commit v1 on v0

v1 whole, which is shorter than its diff:
```python
import functools

import jax
import jax.numpy as jnp
from jax import lax
from jax.experimental import pallas as pl
from jax.experimental.pallas import tpu as pltpu
from jax.sharding import PartitionSpec as P

PARTS = 1
MESH = pl.DeviceIdType.MESH


def passed_along(block, axis, distance):
    devices = range(lax.axis_size(axis))
    route = [(i - distance, i) for i in devices if i - distance in devices]
    return lax.ppermute(block, axis, route)


def contract(data_rows, matrix_rows):
    return lax.dot_general(
        data_rows, matrix_rows, (((1,), (1,)), ((), ())), preferred_element_type=jnp.float32
    )


def early_rounds(own_down, own_up, down_transfer, up_transfer, rounds):
    height = down_transfer.shape[1]
    down_tile = down_transfer[0].reshape(height, -1)
    up_tile = up_transfer[0].reshape(height, -1)

    def gain(trace, distance, tile):
        moved = passed_along(trace.astype(jnp.bfloat16), "layer", distance)
        pieces = lax.all_gather(moved, "row", axis=1, tiled=True)
        return lax.psum_scatter(contract(pieces, tile), "col", scatter_dimension=1, tiled=True)

    def one(counter, carried):
        down_now, up_now = carried
        return own_down + gain(down_now, 1, down_tile), own_up + gain(up_now, -1, up_tile)

    return lax.fori_loop(0, rounds, one, (own_down, own_up))


def kernel(
    layers, rows, cols,
    down_ref, up_ref, wdown_ref, wup_ref, wreflect_ref, out_ref,
    down_v, up_v, stage_t, stage_r, wide, mat_t, mat_r,
    send_down, send_up, xbuf, part1, rs1, own1, summed, gbuf, part2, rs2, own2,
    load_sem, down_sem, up_sem, x_sem, p1_sem, rs1_sem, g_send_sem, g_sem, p2_sem, rs2_sem,
):
    l, r, c = lax.axis_index("layer"), lax.axis_index("row"), lax.axis_index("col")
    parts, size, width = xbuf.shape[1:]
    groups = stage_t.shape[0] // mat_t.shape[0]
    lane = stage_t.shape[1]

    def dev(layer, row, col):
        return (layer, row, col)

    load_down = pltpu.make_async_copy(down_ref.at[0], down_v, load_sem.at[0])
    load_up = pltpu.make_async_copy(up_ref.at[0], up_v, load_sem.at[1])
    load_down.start()
    load_up.start()
    load_t = pltpu.make_async_copy(wdown_ref, stage_t, load_sem.at[2])
    load_tu = pltpu.make_async_copy(wup_ref, stage_t, load_sem.at[2])
    load_r = pltpu.make_async_copy(wreflect_ref, stage_r, load_sem.at[3])

    @pl.when(l == 0)
    def _():
        load_tu.start()

    @pl.when(l == layers - 1)
    def _():
        load_t.start()

    load_r.start()

    barrier = pltpu.get_barrier_semaphore()

    def greet(layer, row, col):
        pl.semaphore_signal(barrier, inc=1, device_id=dev(layer, row, col), device_id_type=MESH)

    for d in range(1, cols):
        greet(l, r, lax.rem(c + d, cols))
    for d in range(1, rows):
        greet(l, lax.rem(r + d, rows), c)
    if layers == 2:
        for d in range(rows):
            greet(1 - l, lax.rem(r + d, rows), c)
        neighbours = 1
    else:
        @pl.when(l > 0)
        def _():
            for d in range(rows):
                greet(l - 1, lax.rem(r + d, rows), c)

        @pl.when(l < layers - 1)
        def _():
            for d in range(rows):
                greet(l + 1, lax.rem(r + d, rows), c)

        neighbours = jnp.where(l > 0, 1, 0) + jnp.where(l < layers - 1, 1, 0)

    load_down.wait()
    load_up.wait()
    for h in range(parts):
        send_down[h] = down_v[h * size:(h + 1) * size].astype(jnp.bfloat16)
        send_up[h] = up_v[h * size:(h + 1) * size].astype(jnp.bfloat16)
    pl.semaphore_wait(barrier, rows * neighbours + (rows - 1) + (cols - 1))

    order = sorted(range(rows), key=lambda d: (abs(d - rows // 2), -d))

    def source_copies(buffer, sems, layer):
        return [
            pltpu.make_async_remote_copy(
                src_ref=buffer.at[h],
                dst_ref=xbuf.at[r, h],
                send_sem=sems.at[h, d],
                recv_sem=x_sem.at[r, h],
                device_id=dev(layer, lax.rem(r + d, rows), c),
                device_id_type=MESH,
            )
            for h in range(parts)
            for d in order
        ]

    @pl.when(l == layers - 2)
    def _():
        for copy in source_copies(send_down, down_sem, l + 1):
            copy.start()

    @pl.when(l == 1)
    def _():
        for copy in source_copies(send_up, up_sem, l - 1):
            copy.start()

    def relayout(stage, mat):
        step = wide.shape[0] // groups

        def one(i, carry):
            wide[...] = stage[pl.ds(pl.multiple_of(i * step * groups, 128), step * groups), :].astype(jnp.float32)
            blocks = groups * lane // width
            for g in range(groups):
                half, b = divmod(g, blocks)
                column = b * width + half * lane
                mat[pl.ds(pl.multiple_of(i * step, 128), step), column:column + lane] = wide[
                    pl.ds(g, step, stride=groups), :
                ].astype(jnp.bfloat16)
            return carry

        lax.fori_loop(0, mat.shape[0] // step, one, 0)

    def far_first(i):
        low = 2 * c < cols - 1
        down_t = cols - 1 - i
        down_t = jnp.where(down_t <= c, down_t - 1, down_t)
        up_t = jnp.where(c <= i, i + 1, i)
        return jnp.where(low, down_t, up_t)

    def product(source, h, mat, target):
        begin = pl.multiple_of(target * width, 128)
        total = None
        for b in range(rows):
            term = contract(source[b, h], mat[pl.ds(begin, width), b * width:(b + 1) * width])
            total = term if total is None else total + term
        return total

    def scatter_copy(h, i, part, sems, landing, landing_sem):
        return pltpu.make_async_remote_copy(
            src_ref=part.at[h, i],
            dst_ref=landing.at[c, h],
            send_sem=sems.at[h, i],
            recv_sem=landing_sem.at[c, h],
            device_id=dev(l, r, far_first(i)),
            device_id_type=MESH,
        )

    def scatter(source, h, mat, part, sems, landing, landing_sem, own):
        for i in range(cols - 1):
            part[h, i] = product(source, h, mat, far_first(i)).astype(jnp.bfloat16)
            scatter_copy(h, i, part, sems, landing, landing_sem).start()
        own[h] = product(source, h, mat, c)

    def arrived(landing, landing_sem, index, h, part):
        pltpu.make_async_remote_copy(
            src_ref=landing.at[index, h],
            dst_ref=landing.at[index, h],
            send_sem=p1_sem.at[0, 0],
            recv_sem=landing_sem.at[index, h],
            device_id=dev(l, r, lax.rem(c + 1, cols)),
            device_id_type=MESH,
        ).wait_recv()

    def collected(h, own, landing, landing_sem):
        total = own[h]
        for d in range(1, cols):
            sender = lax.rem(c + d, cols)
            arrived(landing, landing_sem, sender, h, None)
            total = total + landing[sender, h].astype(jnp.float32)
        return total

    def receives(body):
        if layers == 2:
            body()
        else:
            pl.when((l == 0) | (l == layers - 1))(body)

    @receives
    def _():
        load_t.wait()
        relayout(stage_t, mat_t)
        for h in range(parts):
            for b in range(rows):
                arrived(xbuf, x_sem, b, h, None)
            scatter(xbuf, h, mat_t, part1, p1_sem, rs1, rs1_sem, own1)

    load_r.wait()
    relayout(stage_r, mat_r)

    def gather_copy(h, d):
        return pltpu.make_async_remote_copy(
            src_ref=gbuf.at[r, h],
            dst_ref=gbuf.at[r, h],
            send_sem=g_send_sem.at[h, d],
            recv_sem=g_sem.at[r, h],
            device_id=dev(l, lax.rem(r + d, rows), c),
            device_id_type=MESH,
        )

    gather_order = [d for d in order if d > 0]
    for h in range(parts):
        summed[h] = down_v[h * size:(h + 1) * size] + up_v[h * size:(h + 1) * size]

        @receives
        def _():
            summed[h] = summed[h] + collected(h, own1, rs1, rs1_sem)

        gbuf[r, h] = summed[h].astype(jnp.bfloat16)
        for d in gather_order:
            gather_copy(h, d).start()

    for h in range(parts):
        for d in range(1, rows):
            arrived(gbuf, g_sem, lax.rem(r + d, rows), h, None)
        scatter(gbuf, h, mat_r, part2, p2_sem, rs2, rs2_sem, own2)

    for h in range(parts):
        out_ref[0, h * size:(h + 1) * size] = summed[h] + collected(h, own2, rs2, rs2_sem)

    @pl.when(l == layers - 2)
    def _():
        for copy in source_copies(send_down, down_sem, l + 1):
            copy.wait_send()

    @pl.when(l == 1)
    def _():
        for copy in source_copies(send_up, up_sem, l - 1):
            copy.wait_send()

    for h in range(parts):
        for i in range(cols - 1):
            @receives
            def _():
                scatter_copy(h, i, part1, p1_sem, rs1, rs1_sem).wait_send()

            scatter_copy(h, i, part2, p2_sem, rs2, rs2_sem).wait_send()
        for d in gather_order:
            gather_copy(h, d).wait_send()


def on_device(down_source, up_source, down_transfer, up_transfer, reflection):
    layers, rows, cols = (lax.axis_size(a) for a in ("layer", "row", "col"))
    own_down, own_up = down_source, up_source
    if layers > 2:
        layer = lax.axis_index("layer")
        down_now, up_now = early_rounds(
            own_down[0], own_up[0], down_transfer, up_transfer, layers - 2
        )
        own_down = jnp.where(layer == layers - 1, own_down, down_now[None])
        own_up = jnp.where(layer == 0, own_up, up_now[None])

    _, sources, width = down_source.shape
    _, height, blocks, piece = down_transfer.shape
    lane = 128
    halves = piece // lane
    groups = halves * blocks

    def tiles(w):
        return w.reshape(height, blocks, halves, lane).transpose(0, 2, 1, 3).reshape(-1, lane)

    parts = PARTS
    size = sources // parts
    any_space = pl.BlockSpec(memory_space=pl.ANY)
    vmem = pltpu.VMEM
    f32, bf16 = jnp.float32, jnp.bfloat16
    dma = pltpu.SemaphoreType.DMA
    step = min(height, 256)
    return pl.pallas_call(
        functools.partial(kernel, layers, rows, cols),
        out_shape=jax.ShapeDtypeStruct(down_source.shape, f32),
        in_specs=[any_space] * 5,
        out_specs=pl.BlockSpec(memory_space=pltpu.VMEM),
        scratch_shapes=[
            vmem((sources, width), f32),
            vmem((sources, width), f32),
            vmem((height * groups, lane), bf16),
            vmem((height * groups, lane), bf16),
            vmem((step * groups, lane), f32),
            vmem((height, blocks * piece), bf16),
            vmem((height, blocks * piece), bf16),
            vmem((parts, size, width), bf16),
            vmem((parts, size, width), bf16),
            vmem((rows, parts, size, width), bf16),
            vmem((parts, cols - 1, size, width), bf16),
            vmem((cols, parts, size, width), bf16),
            vmem((parts, size, width), f32),
            vmem((parts, size, width), f32),
            vmem((rows, parts, size, width), bf16),
            vmem((parts, cols - 1, size, width), bf16),
            vmem((cols, parts, size, width), bf16),
            vmem((parts, size, width), f32),
            dma((4,)),
            dma((parts, rows)),
            dma((parts, rows)),
            dma((rows, parts)),
            dma((parts, cols - 1)),
            dma((cols, parts)),
            dma((parts, rows)),
            dma((rows, parts)),
            dma((parts, cols - 1)),
            dma((cols, parts)),
        ],
        compiler_params=pltpu.CompilerParams(collective_id=0, has_side_effects=True),
    )(own_down, own_up, tiles(down_transfer), tiles(up_transfer), tiles(reflection))


def solution(mesh):
    in_specs = (
        P("layer", None, ("row", "col")),
        P("layer", None, ("row", "col")),
        P("layer", "row", None, "col"),
        P("layer", "row", None, "col"),
        P("layer", "row", None, "col"),
    )
    out_specs = P("layer", None, ("row", "col"))
    return jax.shard_map(
        on_device, mesh=mesh, in_specs=in_specs, out_specs=out_specs, check_vma=False
    )
```

time: 97.4 us -> 25.5 us (0.26)
  waiting for transfers between devices: 49 us -> 0 us
  Pallas kernels: 0 us -> 23.9 us
  blocking collectives: 16.4 us -> 0 us
  between operations: 13.2 us -> 0.01 us
  starting transfers between devices: 6.24 us -> 0 us
  matrix products: 4.35 us -> 0 us
  local copies, waits for them, and re-layouts: 4.71 us -> 1.47 us
  other arithmetic: 3.13 us -> 0 us
    reduce_scatter x3 -> x0, waiting for transfers between devices: 44.9 us -> none  [the longest x1 20.5 us: sweep_product(): lax.psum_scatter(contract(pieces[1], up_tile), 'col', scatter_dimension=1...]
    pallas_call x0 -> x1, Pallas kernels: none -> 23.9 us  [on_device(): pl.pallas_call(functools.partial(kernel, layers, rows, cols), out_shape=j...]
    all_gather x3 -> x0, blocking collectives: 16.4 us -> none  [the longest x2 11 us: sweep_product(): lax.all_gather(a, 'row', axis=1, tiled=True)]
    ppermute x2 -> x0, starting transfers between devices: 6.15 us -> none  [passed_along(): return lax.ppermute(block, axis, route)]
    dot_general x3 -> x0, matrix products: 4.35 us -> none  [contract(): lax.dot_general(data_rows, matrix_rows, (((1,), (1,)), ((), ())), preferr...]
    ppermute x2 -> x0, waiting for transfers between devices: 4.01 us -> none  [passed_along(): return lax.ppermute(block, axis, route)]
    unnamed x9 -> x1, local copies, waits for them, and re-layouts: 4.71 us -> 1.47 us
    convert_element_type x3 -> x0, other arithmetic: 1.74 us -> none  [the longest x1 0.89 us: on_device(): mixed_trace = summed.astype(jnp.bfloat16)]
  transfers between devices with their start and end apart: 5 -> 0, of which waited for: 4 -> 0; matrix products, arithmetic and copies ran while one was open for 6% -> 0% of each run, Pallas kernels for 0% -> 0%
where the time goes in v1:
time: 25.5 us; the launch traced here: 25.3 us
  Pallas kernels  23.9 us (94%)
  local copies, waits for them, and re-layouts  1.47 us (6%)
    pallas_call x1, Pallas kernels, on_device(): pl.pallas_call(functools.partial(kernel, layers, rows, cols), out_shape=j...  23.9 us
    unnamed x1, local copies, waits for them, and re-layouts  1.47 us

profile of v1, /device:TPU:0, one launch (start us, length us, event | category | flops | bytes accessed | tf_op | source)
XLA Modules:
  0.0 25.3 jit_solution(16783456942989024980)
XLA Ops:
  0.0 23.9 %shard_map.55 = f32[1,64,256]{2,1,0:T(8,128)} custom-call(f32[1,64,256]{2,1,0:T(8,128)} %down_ref.1, f32[1,64,256]{2,1,0:T(8,128)} %up_ref.1, bf16[8192,128]{1,0:T(8,128)(2,1)} %bitcast.15, bf16[8192,128]{1,0:T(8,128)(2,1)} %bitcast.16, bf16[8192,128]{1,0:T(8,128)(2,1)} %bitcast.17), custom_call_target="tpu_custom_call" | custom-call | tf_op jit(solution)/shard_map/pallas_call | solution.py:296
  23.9 1.5 %copy.10 = f32[1,64,256]{2,1,0:T(8,128)} copy(f32[1,64,256]{2,1,0:T(8,128)} %shard_map.55) | data formatting | bytes 131072

commit v2 on v1

--- a/solution.py
+++ b/solution.py
@@ -295,7 +295,7 @@
     step = min(height, 256)
     return pl.pallas_call(
         functools.partial(kernel, layers, rows, cols),
-        out_shape=jax.ShapeDtypeStruct(down_source.shape, f32),
+        out_shape=pltpu.VMEM(down_source.shape, f32),
         in_specs=[any_space] * 5,
         out_specs=pl.BlockSpec(memory_space=pltpu.VMEM),
         scratch_shapes=[

time: 25.5 us -> 24 us (0.941)
  local copies, waits for them, and re-layouts: 1.47 us -> 0.63 us
  Pallas kernels: 23.9 us -> 23.2 us
    unnamed x1, local copies, waits for them, and re-layouts: 1.47 us -> 0.63 us
    pallas_call x1, Pallas kernels: 23.9 us -> 23.2 us  [on_device(): pl.pallas_call(functools.partial(kernel, layers, rows, cols), out_shape=p...]
where the time goes in v2:
time: 24 us; the launch traced here: 23.9 us
  Pallas kernels  23.2 us (97%)
  local copies, waits for them, and re-layouts  0.63 us (3%)
    pallas_call x1, Pallas kernels, on_device(): pl.pallas_call(functools.partial(kernel, layers, rows, cols), out_shape=p...  23.2 us
    unnamed x1, local copies, waits for them, and re-layouts  0.63 us

profile of v2, /device:TPU:0, one launch (start us, length us, event | category | flops | bytes accessed | tf_op | source)
XLA Modules:
  0.0 23.9 jit_solution(10311389145910827930)
XLA Ops:
  0.0 23.2 %shard_map.55 = f32[1,64,256]{2,1,0:T(8,128)S(1)} custom-call(f32[1,64,256]{2,1,0:T(8,128)} %down_ref.1, f32[1,64,256]{2,1,0:T(8,128)} %up_ref.1, bf16[8192,128]{1,0:T(8,128)(2,1)} %bitcast.15, bf16[8192,128]{1,0:T(8,128)(2,1)} %bitcast.16, bf16[8192,128]{1,0:T(8,128)(2,1)} %bitcast.17), custom_call_target="tpu_custom_call" | custom-call | tf_op jit(solution)/shard_map/pallas_call | solution.py:296
  23.2 0.6 %copy.10 = f32[1,64,256]{2,1,0:T(8,128)} copy(f32[1,64,256]{2,1,0:T(8,128)S(1)} %shard_map.55) | data formatting | bytes 131072

commit v3 on v2

--- a/solution.py
+++ b/solution.py
@@ -46,6 +46,7 @@
     down_v, up_v, stage_t, stage_r, wide, mat_t, mat_r,
     send_down, send_up, xbuf, part1, rs1, own1, summed, gbuf, part2, rs2, own2,
     load_sem, down_sem, up_sem, x_sem, p1_sem, rs1_sem, g_send_sem, g_sem, p2_sem, rs2_sem,
+    relay_sem, far_sem,
 ):
     l, r, c = lax.axis_index("layer"), lax.axis_index("row"), lax.axis_index("col")
     parts, size, width = xbuf.shape[1:]
@@ -54,6 +55,44 @@
 
     def dev(layer, row, col):
         return (layer, row, col)
+
+    order = sorted(range(rows), key=lambda d: (abs(d - rows // 2), -d))
+    partner = r + 1 - 2 * lax.rem(r, 2)
+
+    barrier = pltpu.get_barrier_semaphore()
+
+    def greet(layer, row, col):
+        pl.semaphore_signal(barrier, inc=1, device_id=dev(layer, row, col), device_id_type=MESH)
+
+    source_order = [d for d in order if d % 2 == 0]
+    if layers == 2:
+        for d in source_order:
+            greet(1 - l, lax.rem(r + d, rows), c)
+        neighbours = 1
+    else:
+        @pl.when(l > 0)
+        def _():
+            for d in source_order:
+                greet(l - 1, lax.rem(r + d, rows), c)
+
+        @pl.when(l < layers - 1)
+        def _():
+            for d in source_order:
+                greet(l + 1, lax.rem(r + d, rows), c)
+
+        neighbours = jnp.where(l > 0, 1, 0) + jnp.where(l < layers - 1, 1, 0)
+
+    @pl.when(c > 0)
+    def _():
+        greet(l, r, c - 1)
+
+    @pl.when(c < cols - 1)
+    def _():
+        greet(l, r, c + 1)
+
+    beside = jnp.where(c > 0, 1, 0) + jnp.where(c < cols - 1, 1, 0)
+    for d in range(1, rows):
+        greet(l, lax.rem(r + d, rows), c)
 
     load_down = pltpu.make_async_copy(down_ref.at[0], down_v, load_sem.at[0])
     load_up = pltpu.make_async_copy(up_ref.at[0], up_v, load_sem.at[1])
@@ -73,40 +112,12 @@
 
     load_r.start()
 
-    barrier = pltpu.get_barrier_semaphore()
-
-    def greet(layer, row, col):
-        pl.semaphore_signal(barrier, inc=1, device_id=dev(layer, row, col), device_id_type=MESH)
-
-    for d in range(1, cols):
-        greet(l, r, lax.rem(c + d, cols))
-    for d in range(1, rows):
-        greet(l, lax.rem(r + d, rows), c)
-    if layers == 2:
-        for d in range(rows):
-            greet(1 - l, lax.rem(r + d, rows), c)
-        neighbours = 1
-    else:
-        @pl.when(l > 0)
-        def _():
-            for d in range(rows):
-                greet(l - 1, lax.rem(r + d, rows), c)
-
-        @pl.when(l < layers - 1)
-        def _():
-            for d in range(rows):
-                greet(l + 1, lax.rem(r + d, rows), c)
-
-        neighbours = jnp.where(l > 0, 1, 0) + jnp.where(l < layers - 1, 1, 0)
-
     load_down.wait()
     load_up.wait()
     for h in range(parts):
         send_down[h] = down_v[h * size:(h + 1) * size].astype(jnp.bfloat16)
         send_up[h] = up_v[h * size:(h + 1) * size].astype(jnp.bfloat16)
-    pl.semaphore_wait(barrier, rows * neighbours + (rows - 1) + (cols - 1))
-
-    order = sorted(range(rows), key=lambda d: (abs(d - rows // 2), -d))
+    pl.semaphore_wait(barrier, len(source_order) * neighbours + (rows - 1) + beside)
 
     def source_copies(buffer, sems, layer):
         return [
@@ -119,7 +130,7 @@
                 device_id_type=MESH,
             )
             for h in range(parts)
-            for d in order
+            for d in source_order
         ]
 
     @pl.when(l == layers - 2)
@@ -131,6 +142,29 @@
     def _():
         for copy in source_copies(send_up, up_sem, l - 1):
             copy.start()
+
+    def tell(hop, side, col):
+        pl.semaphore_signal(
+            far_sem.at[side, hop], inc=1, device_id=dev(l, r, col), device_id_type=MESH
+        )
+
+    def known(hop):
+        for side, sign in ((0, -1), (1, 1)):
+            there = (c >= hop) if sign < 0 else (c < cols - hop)
+            onward = (c < cols - 1) if sign < 0 else (c > 0)
+
+            if hop > 1:
+                @pl.when(there)
+                def _():
+                    pl.semaphore_wait(far_sem.at[side, hop], 1)
+
+            if hop < cols - 1:
+                @pl.when(there & onward)
+                def _():
+                    tell(hop + 1, side, c - sign)
+
+    for hop in range(1, cols - 1):
+        known(hop)
 
     def relayout(stage, mat):
         step = wide.shape[0] // groups
@@ -179,7 +213,7 @@
             scatter_copy(h, i, part, sems, landing, landing_sem).start()
         own[h] = product(source, h, mat, c)
 
-    def arrived(landing, landing_sem, index, h, part):
+    def arrived(landing, landing_sem, index, h):
         pltpu.make_async_remote_copy(
             src_ref=landing.at[index, h],
             dst_ref=landing.at[index, h],
@@ -193,9 +227,20 @@
         total = own[h]
         for d in range(1, cols):
             sender = lax.rem(c + d, cols)
-            arrived(landing, landing_sem, sender, h, None)
+            arrived(landing, landing_sem, sender, h)
             total = total + landing[sender, h].astype(jnp.float32)
         return total
+
+    def relay_copy(h, d):
+        b = lax.rem(r + d, rows)
+        return pltpu.make_async_remote_copy(
+            src_ref=xbuf.at[b, h],
+            dst_ref=xbuf.at[b, h],
+            send_sem=relay_sem.at[h, d],
+            recv_sem=x_sem.at[b, h],
+            device_id=dev(l, partner, c),
+            device_id_type=MESH,
+        )
 
     def receives(body):
         if layers == 2:
@@ -207,9 +252,17 @@
     def _():
         load_t.wait()
         relayout(stage_t, mat_t)
+
+    known(cols - 1)
+
+    @receives
+    def _():
         for h in range(parts):
-            for b in range(rows):
-                arrived(xbuf, x_sem, b, h, None)
+            for d in source_order:
+                arrived(xbuf, x_sem, lax.rem(r + d, rows), h)
+                relay_copy(h, d).start()
+            for d in source_order:
+                arrived(xbuf, x_sem, lax.rem(partner + d, rows), h)
             scatter(xbuf, h, mat_t, part1, p1_sem, rs1, rs1_sem, own1)
 
     load_r.wait()
@@ -239,7 +292,7 @@
 
     for h in range(parts):
         for d in range(1, rows):
-            arrived(gbuf, g_sem, lax.rem(r + d, rows), h, None)
+            arrived(gbuf, g_sem, lax.rem(r + d, rows), h)
         scatter(gbuf, h, mat_r, part2, p2_sem, rs2, rs2_sem, own2)
 
     for h in range(parts):
@@ -264,6 +317,11 @@
             scatter_copy(h, i, part2, p2_sem, rs2, rs2_sem).wait_send()
         for d in gather_order:
             gather_copy(h, d).wait_send()
+
+        @receives
+        def _():
+            for d in source_order:
+                relay_copy(h, d).wait_send()
 
 
 def on_device(down_source, up_source, down_transfer, up_transfer, reflection):
@@ -327,6 +385,8 @@
             dma((rows, parts)),
             dma((parts, cols - 1)),
             dma((cols, parts)),
+            dma((parts, rows)),
+            pltpu.SemaphoreType.REGULAR((2, cols)),
         ],
         compiler_params=pltpu.CompilerParams(collective_id=0, has_side_effects=True),
     )(own_down, own_up, tiles(down_transfer), tiles(up_transfer), tiles(reflection))

time: 24 us -> 23.2 us (0.967)
  Pallas kernels: 23.2 us -> 22.4 us
    pallas_call x1, Pallas kernels: 23.2 us -> 22.4 us  [on_device(): pl.pallas_call(functools.partial(kernel, layers, rows, cols), out_shape=p...]
where the time goes in v3:
time: 23.2 us; the launch traced here: 23 us
  Pallas kernels  22.4 us (97%)
  local copies, waits for them, and re-layouts  0.63 us (3%)
    pallas_call x1, Pallas kernels, on_device(): pl.pallas_call(functools.partial(kernel, layers, rows, cols), out_shape=p...  22.4 us
    unnamed x1, local copies, waits for them, and re-layouts  0.63 us

profile of v3, /device:TPU:0, one launch (start us, length us, event | category | flops | bytes accessed | tf_op | source)
XLA Modules:
  0.0 23.0 jit_solution(6531562463537696833)
XLA Ops:
  0.0 22.4 %shard_map.55 = f32[1,64,256]{2,1,0:T(8,128)S(1)} custom-call(f32[1,64,256]{2,1,0:T(8,128)} %down_ref.1, f32[1,64,256]{2,1,0:T(8,128)} %up_ref.1, bf16[8192,128]{1,0:T(8,128)(2,1)} %bitcast.15, bf16[8192,128]{1,0:T(8,128)(2,1)} %bitcast.16, bf16[8192,128]{1,0:T(8,128)(2,1)} %bitcast.17), custom_call_target="tpu_custom_call" | custom-call | tf_op jit(solution)/shard_map/pallas_call | solution.py:354
  22.4 0.6 %copy.10 = f32[1,64,256]{2,1,0:T(8,128)} copy(f32[1,64,256]{2,1,0:T(8,128)S(1)} %shard_map.55) | data formatting | bytes 131072

commit v4 on v3

--- a/solution.py
+++ b/solution.py
@@ -7,6 +7,8 @@
 from jax.experimental.pallas import tpu as pltpu
 from jax.sharding import PartitionSpec as P
 
+EARLY = 1
+ORD = 0
 PARTS = 1
 MESH = pl.DeviceIdType.MESH
 
@@ -46,7 +48,7 @@
     down_v, up_v, stage_t, stage_r, wide, mat_t, mat_r,
     send_down, send_up, xbuf, part1, rs1, own1, summed, gbuf, part2, rs2, own2,
     load_sem, down_sem, up_sem, x_sem, p1_sem, rs1_sem, g_send_sem, g_sem, p2_sem, rs2_sem,
-    relay_sem, far_sem,
+    early, relay_sem, far_sem,
 ):
     l, r, c = lax.axis_index("layer"), lax.axis_index("row"), lax.axis_index("col")
     parts, size, width = xbuf.shape[1:]
@@ -183,17 +185,22 @@
         lax.fori_loop(0, mat.shape[0] // step, one, 0)
 
     def far_first(i):
+        if ORD == 1:
+            i = cols - 2 - i
+        if ORD == 2:
+            return lax.rem(c + 2 + i, cols) if i < 2 else lax.rem(c + 1, cols)
         low = 2 * c < cols - 1
         down_t = cols - 1 - i
         down_t = jnp.where(down_t <= c, down_t - 1, down_t)
         up_t = jnp.where(c <= i, i + 1, i)
         return jnp.where(low, down_t, up_t)
 
-    def product(source, h, mat, target):
+    def product(source, h, mat, target, blocks):
         begin = pl.multiple_of(target * width, 128)
         total = None
-        for b in range(rows):
-            term = contract(source[b, h], mat[pl.ds(begin, width), b * width:(b + 1) * width])
+        for b in blocks:
+            column = b * width if isinstance(b, int) else pl.multiple_of(b * width, 128)
+            term = contract(source[b, h], mat[pl.ds(begin, width), pl.ds(column, width)])
             total = term if total is None else total + term
         return total
 
@@ -207,11 +214,23 @@
             device_id_type=MESH,
         )
 
-    def scatter(source, h, mat, part, sems, landing, landing_sem, own):
-        for i in range(cols - 1):
-            part[h, i] = product(source, h, mat, far_first(i)).astype(jnp.bfloat16)
-            scatter_copy(h, i, part, sems, landing, landing_sem).start()
-        own[h] = product(source, h, mat, c)
+    def scatter(source, source_sem, first, rest, h, mat, part, sems, landing, landing_sem, own):
+        targets = [far_first(i) for i in range(cols - 1)] + [c]
+        if first:
+            for i, target in enumerate(targets):
+                early[i] = product(source, h, mat, target, first)
+        for b in rest:
+            arrived(source, source_sem, b, h)
+        for i, target in enumerate(targets):
+            if first:
+                total = early[i] + product(source, h, mat, target, rest)
+            else:
+                total = product(source, h, mat, target, range(rows))
+            if i < cols - 1:
+                part[h, i] = total.astype(jnp.bfloat16)
+                scatter_copy(h, i, part, sems, landing, landing_sem).start()
+            else:
+                own[h] = total
 
     def arrived(landing, landing_sem, index, h):
         pltpu.make_async_remote_copy(
@@ -261,9 +280,9 @@
             for d in source_order:
                 arrived(xbuf, x_sem, lax.rem(r + d, rows), h)
                 relay_copy(h, d).start()
-            for d in source_order:
-                arrived(xbuf, x_sem, lax.rem(partner + d, rows), h)
-            scatter(xbuf, h, mat_t, part1, p1_sem, rs1, rs1_sem, own1)
+            rest = [lax.rem(partner + d, rows) for d in source_order]
+            first = [lax.rem(r + d, rows) for d in source_order]
+            scatter(xbuf, x_sem, first if EARLY > 1 else [], rest, h, mat_t, part1, p1_sem, rs1, rs1_sem, own1)
 
     load_r.wait()
     relayout(stage_r, mat_r)
@@ -291,9 +310,14 @@
             gather_copy(h, d).start()
 
     for h in range(parts):
-        for d in range(1, rows):
-            arrived(gbuf, g_sem, lax.rem(r + d, rows), h)
-        scatter(gbuf, h, mat_r, part2, p2_sem, rs2, rs2_sem, own2)
+        if EARLY:
+            arrived(gbuf, g_sem, partner, h)
+            first = [r, partner]
+            rest = [lax.rem(r - lax.rem(r, 2) + d, rows) for d in range(2, rows)]
+        else:
+            first = []
+            rest = [lax.rem(r + d, rows) for d in range(1, rows)]
+        scatter(gbuf, g_sem, first, rest, h, mat_r, part2, p2_sem, rs2, rs2_sem, own2)
 
     for h in range(parts):
         out_ref[0, h * size:(h + 1) * size] = summed[h] + collected(h, own2, rs2, rs2_sem)
@@ -385,6 +409,7 @@
             dma((rows, parts)),
             dma((parts, cols - 1)),
             dma((cols, parts)),
+            vmem((cols, size, width), f32),
             dma((parts, rows)),
             pltpu.SemaphoreType.REGULAR((2, cols)),
         ],

time: 23.2 us -> 23 us (level)
  no operation moved by 1% of the time
where the time goes in v4:
time: 23 us; the launch traced here: 22.8 us
  Pallas kernels  22.2 us (97%)
  local copies, waits for them, and re-layouts  0.63 us (3%)
    pallas_call x1, Pallas kernels, on_device(): pl.pallas_call(functools.partial(kernel, layers, rows, cols), out_shape=p...  22.2 us
    unnamed x1, local copies, waits for them, and re-layouts  0.63 us

profile of v4, /device:TPU:0, one launch (start us, length us, event | category | flops | bytes accessed | tf_op | source)
XLA Modules:
  0.0 22.8 jit_solution(17670242215928215849)
XLA Ops:
  0.0 22.2 %shard_map.55 = f32[1,64,256]{2,1,0:T(8,128)S(1)} custom-call(f32[1,64,256]{2,1,0:T(8,128)} %down_ref.1, f32[1,64,256]{2,1,0:T(8,128)} %up_ref.1, bf16[8192,128]{1,0:T(8,128)(2,1)} %bitcast.15, bf16[8192,128]{1,0:T(8,128)(2,1)} %bitcast.16, bf16[8192,128]{1,0:T(8,128)(2,1)} %bitcast.17), custom_call_target="tpu_custom_call" | custom-call | tf_op jit(solution)/shard_map/pallas_call | solution.py:378
  22.2 0.6 %copy.10 = f32[1,64,256]{2,1,0:T(8,128)} copy(f32[1,64,256]{2,1,0:T(8,128)S(1)} %shard_map.55) | data formatting | bytes 131072
